TPU v7x, 32 devices: a whole 2x2x4 slice. The times are simulated.
32 devices in a mesh: rows: 8 (over z, y), cols: 4 (over x, core).
Axes of the slice: x: 2, y: 2, z: 4, core: 2. Of those that a mesh axis runs over, the one named last changes fastest.
Arguments:
- right_leaf: float32 [4, 2048, 128], P(None, 'rows'), may hold values from -6 to 6
- right_mid: float32 [2, 4096, 128], P(None, 'rows'), may hold values from -6 to 6
- right_root: float32 [8192, 128], P('rows'), may hold values from -6 to 6
- inverse_leaf: float32 [4, 2048, 2048], P(None, 'rows', 'cols'), may hold values from -1 to 2, as said below
- inverse_mid: float32 [2, 4096, 4096], P(None, 'rows', 'cols'), may hold values from -1 to 2, as said below
- inverse_root: float32 [8192, 8192], P('rows', 'cols'), may hold values from -1 to 2, as said below
- leaf_to_mid: float32 [4, 4096, 2048], P(None, 'rows', 'cols'), may hold values from -0.125 to 0.125
- leaf_to_root: float32 [4, 8192, 2048], P(None, 'rows', 'cols'), may hold values from -0.125 to 0.125
- mid_to_root: float32 [2, 8192, 4096], P(None, 'rows', 'cols'), may hold values from -0.09375 to 0.09375
- mask_leaf_mid: int32 [4, 32, 16], replicated, may hold values 0 or 1
- mask_leaf_root: int32 [4, 64, 16], replicated, may hold values 0 or 1
- mask_mid_root: int32 [2, 64, 32], replicated, may hold values 0 or 1
Outputs:
- solved_leaf: float32 [4, 2048, 128], P(None, 'rows')
- solved_mid: float32 [2, 4096, 128], P(None, 'rows')
- solved_root: float32 [8192, 128], P('rows')
Inputs may be any that keep to these rules, and one draw needn't show every extreme that they name: `inverse_leaf`: lower triangular, with its diagonal between 0.5 and 2. `inverse_mid`: lower triangular, with its diagonal between 0.5 and 2. `inverse_root`: lower triangular, with its diagonal between 0.5 and 2.
All inputs are finite; a program needn't handle non-finite values.
Results may differ from a plain program's by a relative error of at most 0.00014.
Values sent between devices are 32-bit elements; how exact they have to be, the bound alone decides.
No kernel may reach another device: no remote copies, remote signals or barrier semaphores. Data moves between devices by JAX's collectives and lax.ppermute only.
A program may use at most 128 MiB of HBM per device.

v0:
```python
import jax
import jax.numpy as jnp
from jax import lax
from jax.sharding import PartitionSpec as P

TILE = 128


def product(matrix, vector):
    return jnp.einsum(
        "src,sck->srk",
        matrix,
        vector,
        precision=lax.Precision.HIGHEST,
        preferred_element_type=jnp.float32,
    )


def own_columns(gathered):
    col_width = gathered.shape[1] // lax.axis_size("cols")
    return lax.dynamic_slice_in_dim(gathered, lax.axis_index("cols") * col_width, col_width, 1)


def masked(values, pattern):
    rows_dev = values.shape[1]
    cols_dev = values.shape[2]
    row_ids = lax.axis_index("rows") * rows_dev + lax.iota(jnp.int32, rows_dev)
    col_ids = lax.axis_index("cols") * cols_dev + lax.iota(jnp.int32, cols_dev)
    row_hot = (row_ids[:, None] // TILE == lax.iota(jnp.int32, pattern.shape[1])[None, :]).astype(
        jnp.float32
    )
    col_hot = (col_ids[:, None] // TILE == lax.iota(jnp.int32, pattern.shape[2])[None, :]).astype(
        jnp.float32
    )
    expanded = jnp.einsum("ra,sab,cb->src", row_hot, pattern.astype(jnp.float32), col_hot)
    return values * expanded


def fetch_columns(block):
    gathered = lax.all_gather(block, "rows", axis=1, tiled=True)
    return own_columns(gathered)


def solve_block(residual, inverse, spread_needed):
    partial_value = product(inverse, fetch_columns(residual))
    solved = lax.psum(partial_value, "cols")
    spread = fetch_columns(solved) if spread_needed else solved
    return (solved, spread)


def body(
    right_leaf,
    right_mid,
    right_root,
    inverse_leaf,
    inverse_mid,
    inverse_root,
    leaf_to_mid,
    leaf_to_root,
    mid_to_root,
    mask_leaf_mid,
    mask_leaf_root,
    mask_mid_root,
):
    factor_lm = masked(leaf_to_mid, mask_leaf_mid)
    factor_lr = masked(leaf_to_root, mask_leaf_root)
    factor_mr = masked(mid_to_root, mask_mid_root)
    solved_leaf, leaf_columns = solve_block(right_leaf, inverse_leaf, True)
    mid_terms = product(factor_lm, leaf_columns)
    mid_part = mid_terms.reshape(2, 2, mid_terms.shape[1], mid_terms.shape[2]).sum(axis=1)
    root_part = product(factor_lr, leaf_columns).sum(axis=0)[None]
    mid_summed, root_summed = lax.psum((mid_part, root_part), "cols")
    resid_mid = right_mid - mid_summed
    solved_mid, mid_columns = solve_block(resid_mid, inverse_mid, True)
    root_more = product(factor_mr, mid_columns).sum(axis=0)[None]
    resid_root = right_root[None] - root_summed - lax.psum(root_more, "cols")
    solved_root, unused_spread = solve_block(resid_root, inverse_root[None], False)
    return (solved_leaf, solved_mid, solved_root[0])


def solution(mesh):
    placed = (
        P(None, "rows", None),
        P(None, "rows", None),
        P("rows", None),
        P(None, "rows", "cols"),
        P(None, "rows", "cols"),
        P("rows", "cols"),
        P(None, "rows", "cols"),
        P(None, "rows", "cols"),
        P(None, "rows", "cols"),
        P(),
        P(),
        P(),
    )
    return jax.shard_map(
        body,
        mesh=mesh,
        in_specs=placed,
        out_specs=(P(None, "rows", None), P(None, "rows", None), P("rows", None)),
        check_vma=False,
    )
```

profile of v0, /device:TPU:0, one launch (start us, length us, event | category | flops | bytes accessed | tf_op | source)
XLA Modules:
  0.0 608.7 jit_solution(15092546820964897420)
XLA Ops:
  7.2 0.0 all-gather.6.cloned.1.call-start
  7.2 2.2 copy.32
  9.4 0.0 all-gather.6.cloned.1.call-update
  9.4 0.0 all-reduce.7.cloned.1.call-start
  9.5 78.9 %all-gather.6.cloned.1.call-done = f32[4,2048,128]{1,2,0:T(8,128)} async-done(((f32[4,256,128]{1,2,0:T(8,128)}), f32[4,2048,128]{1,2,0:T(8,128)}) %all-gather.6.cloned.1.call-update) | async-done | bytes 4194320 | tf_op jit(solution)/shard_map/all_gather | solution.py:40
  88.4 4.2 convolution_bitcast_fusion.1
  92.6 0.0 all-reduce.7.cloned.1.call-update
  92.6 0.0 all-gather.8.cloned.1.call-start
  92.7 31.4 %all-reduce.7.cloned.1.call-done = f32[4,256,128]{1,2,0:T(8,128)} async-done(((f32[4,256,128]{1,2,0:T(8,128)}), f32[4,256,128]{1,2,0:T(8,128)}) %all-reduce.7.cloned.1.call-update) | async-done | bytes 524304 | tf_op jit(solution)/shard_map/psum | solution.py:46
  124.1 0.0 all-gather.8.cloned.1.call-update
  124.1 0.0 all-reduce.9.cloned.1.call-start
  124.3 0.2 fusion.32
  124.4 2.7 fusion.37
  127.1 74.1 %all-gather.8.cloned.1.call-done = f32[4,2048,128]{1,2,0:T(8,128)} async-done(((f32[4,256,128]{1,2,0:T(8,128)}), f32[4,2048,128]{1,2,0:T(8,128)}) %all-gather.8.cloned.1.call-update) | async-done | bytes 4194320 | tf_op jit(solution)/shard_map/all_gather | solution.py:40
  201.2 7.5 %bitcast_reduce_fusion = f32[2,512,128]{2,1,0:T(8,128)S(1)} fusion(f32[4,2048,128]{1,2,0:T(8,128)} %all-gather.8.cloned.1.call-done, s32[]{:T(128)S(6)} %select_n.49, f32[4,512,512]{2,1,0:T(8,128)} %param.18, f32[4,512,512]{2,1,0:T(8,128)} %fusion.37), kind=kOutput, calls=%fused_computation.12 | convolution fusion | flops 1611792384 | bytes 9961476 | tf_op jit(solution)/shard_map/src,sck->srk/dot_general | solution.py:10
  208.7 1.0 copy.34
  209.7 0.0 all-reduce.9.cloned.1.call-update
  209.7 0.0 all-gather.10.cloned.1.call-start
  209.8 0.2 copy.35
  210.0 31.2 %all-reduce.9.cloned.1.call-done = f32[2,512,128]{1,2,0:T(8,128)} async-done(((f32[2,512,128]{1,2,0:T(8,128)}), f32[2,512,128]{1,2,0:T(8,128)}) %all-reduce.9.cloned.1.call-update) | async-done | bytes 524304 | tf_op jit(solution)/shard_map/psum | solution.py:72
  241.3 1.9 sub.35
  243.2 0.0 all-gather.10.cloned.1.call-update
  243.2 0.0 all-reduce.11.cloned.1.call-start
  243.3 74.0 %all-gather.10.cloned.1.call-done = f32[2,4096,128]{1,2,0:T(8,128)} async-done(((f32[2,512,128]{1,2,0:T(8,128)}), f32[2,4096,128]{1,2,0:T(8,128)}) %all-gather.10.cloned.1.call-update) | async-done | bytes 4194320 | tf_op jit(solution)/shard_map/all_gather | solution.py:40
  317.3 7.7 %convolution_bitcast_fusion.2 = f32[2,512,128]{1,2,0:T(8,128)} fusion(f32[2,512,1024]{2,1,0:T(8,128)} %param.16, f32[2,4096,128]{1,2,0:T(8,128)} %all-gather.10.cloned.1.call-done, s32[]{:T(128)S(6)} %select_n.52), kind=kOutput, calls=%fused_computation.10 | convolution fusion | flops 1610612736 | bytes 5767172 | tf_op jit(solution)/shard_map/src,sck->srk/dot_general | solution.py:10
  325.0 0.0 all-reduce.11.cloned.1.call-update
  325.0 0.0 all-gather.12.cloned.1.call-start
  325.0 31.5 %all-reduce.11.cloned.1.call-done = f32[2,512,128]{1,2,0:T(8,128)} async-done(((f32[2,512,128]{1,2,0:T(8,128)}), f32[2,512,128]{1,2,0:T(8,128)}) %all-reduce.11.cloned.1.call-update) | async-done | bytes 524304 | tf_op jit(solution)/shard_map/psum | solution.py:46
  356.6 0.0 all-gather.12.cloned.1.call-update
  356.6 0.2 all-reduce.15.cloned.1.call-start
  356.9 0.2 fusion.24
  357.1 0.2 fusion.25
  357.3 1.3 fusion.35
  358.6 4.5 fusion.29
  363.1 8.7 %fusion.6 = f32[1,1024,128]{2,1,0:T(8,128)} fusion(f32[4,1024,512]{2,1,0:T(8,128)S(1)} %bitcast.56, f32[4,1024,512]{2,1,0:T(8,128)S(1)} %fusion.35, f32[4,2048,128]{1,2,0:T(8,128)} %all-gather.8.cloned.1.call-done, s32[]{:T(128)S(6)} %select_n.49), kind=kOutput, calls=%fused_computation.6 | convolution fusion | flops 3223322624 | bytes 18350084 | tf_op jit(solution)/shard_map/src,sck->srk/dot_general | solution.py:10
  371.9 60.3 %all-gather.12.cloned.1.call-done = f32[2,4096,128]{1,2,0:T(8,128)} async-done(((f32[2,512,128]{1,2,0:T(8,128)}), f32[2,4096,128]{1,2,0:T(8,128)}) %all-gather.12.cloned.1.call-update) | async-done | bytes 4194320 | tf_op jit(solution)/shard_map/all_gather | solution.py:40
  432.2 11.2 %fusion.9 = f32[1,1024,128]{2,1,0:T(8,128)} fusion(f32[2,1024,1024]{2,1,0:T(8,128)} %param.20, f32[2,1024,1024]{2,1,0:T(8,128)} %fusion.29, f32[2,4096,128]{1,2,0:T(8,128)} %all-gather.12.cloned.1.call-done, s32[]{:T(128)S(6)} %select_n.52), kind=kOutput, calls=%fused_computation.7 | convolution fusion | flops 3223322624 | bytes 18350084 | tf_op jit(solution)/shard_map/src,sck->srk/dot_general | solution.py:10
  443.4 0.0 all-reduce.15.cloned.1.call-update
  443.5 0.0 all-gather.14.cloned.1.call-start
  443.5 34.5 %all-reduce.15.cloned.1.call-done = (f32[1,1024,128]{2,1,0:T(8,128)}, f32[1,1024,128]{2,1,0:T(8,128)}) async-done(((f32[1,1024,128]{2,1,0:T(8,128)}, f32[1,1024,128]{2,1,0:T(8,128)}), (f32[1,1024,128]{2,1,0:T(8,128)}, f32[1,1024,128]{2,1,0:T(8,128)})) %all-reduce.15.cloned.1.call-update) | async-done | bytes 1048592 | tf_op jit(solution)/shard_map/psum | solution.py:76
  478.1 2.1 fusion.23
  480.2 0.0 all-reduce.13.cloned.1.call-start
  480.2 74.6 %all-gather.14.cloned.1.call-done = f32[1,8192,128]{2,1,0:T(8,128)} async-done(((f32[1,1024,128]{2,1,0:T(8,128)}), f32[1,8192,128]{2,1,0:T(8,128)}) %all-gather.14.cloned.1.call-update) | async-done | bytes 4194320 | tf_op jit(solution)/shard_map/all_gather | solution.py:40
  554.8 13.4 %convolution_bitcast_fusion = f32[1024,128]{0,1:T(8,128)} fusion(f32[1024,2048]{1,0:T(8,128)} %param.17, f32[1,8192,128]{2,1,0:T(8,128)} %all-gather.14.cloned.1.call-done, s32[]{:T(128)S(6)} %select_n.55), kind=kOutput, calls=%fused_computation.8 | convolution fusion | flops 3221225472 | bytes 9961476 | tf_op jit(solution)/shard_map/src,sck->srk/dot_general | solution.py:10
  568.3 1.0 copy.38
  569.3 1.0 copy.39
  570.3 29.6 %all-reduce.13.cloned.1.call-done = f32[1024,128]{0,1:T(8,128)} async-done(((f32[1024,128]{0,1:T(8,128)}), f32[1024,128]{0,1:T(8,128)}) %all-reduce.13.cloned.1.call-update) | async-done | bytes 524304 | tf_op jit(solution)/shard_map/psum | solution.py:46
  599.9 2.0 copy.40
  (32 shorter events, 0.2 us)
Async XLA Ops:
  7.2 81.2 %copy-start = (f32[4,256,512]{2,1,0:T(8,128)S(1)}, f32[4,256,512]{2,1,0:T(8,128)}, u32[]{:S(2)}) copy-start(f32[4,256,512]{2,1,0:T(8,128)} %param.15) | copy-start | bytes 6291460
  7.2 117.0 %copy-start.6 = (s32[4,32,16]{1,2,0:T(8,128)S(1)}, s32[4,32,16]{1,2,0:T(8,128)}, u32[]{:S(2)}) copy-start(s32[4,32,16]{1,2,0:T(8,128)} %param.21) | copy-start | bytes 24580
  7.2 81.2 %all-gather.6.cloned.1.call-start = ((), (), s32[]{:S(2)}) async-start(), calls=%async_computation | async-start | bytes 4718592 | tf_op jit(solution)/shard_map/all_gather | solution.py:40
  9.4 114.7 %all-reduce.7.cloned.1.call-start = ((), (), s32[]{:S(2)}) async-start(), calls=%async_computation.1 | async-start | bytes 1048576 | tf_op jit(solution)/shard_map/psum | solution.py:46
  92.6 108.6 %all-gather.8.cloned.1.call-start = ((), (), s32[]{:S(2)}) async-start(), calls=%async_computation.2 | async-start | bytes 4718592 | tf_op jit(solution)/shard_map/all_gather | solution.py:40
  124.1 117.1 %all-reduce.9.cloned.1.call-start = ((), (), s32[]{:S(2)}) async-start(), calls=%async_computation.3 | async-start | bytes 1048576 | tf_op jit(solution)/shard_map/psum | solution.py:72
  127.1 82.7 %copy-start.4 = (f32[2,512,128]{2,1,0:T(8,128)S(1)}, f32[2,512,128]{2,1,0:T(8,128)}, u32[]{:S(2)}) copy-start(f32[2,512,128]{2,1,0:T(8,128)} %param.13) | copy-start | bytes 1572868
  209.7 107.5 %all-gather.10.cloned.1.call-start = ((), (), s32[]{:S(2)}) async-start(), calls=%async_computation.4 | async-start | bytes 4718592 | tf_op jit(solution)/shard_map/all_gather | solution.py:40
  210.0 146.8 %copy-start.7 = (s32[2,64,32]{1,2,0:T(8,128)S(1)}, s32[2,64,32]{1,2,0:T(8,128)}, u32[]{:S(2)}) copy-start(s32[2,64,32]{1,2,0:T(8,128)} %param.23) | copy-start | bytes 49156
  210.0 146.8 %copy-start.8 = (s32[4,64,16]{1,2,0:T(8,128)S(1)}, s32[4,64,16]{1,2,0:T(8,128)}, u32[]{:S(2)}) copy-start(s32[4,64,16]{1,2,0:T(8,128)} %param.22) | copy-start | bytes 49156
  243.2 113.4 %all-reduce.11.cloned.1.call-start = ((), (), s32[]{:S(2)}) async-start(), calls=%async_computation.5 | async-start | bytes 1048576 | tf_op jit(solution)/shard_map/psum | solution.py:46
  325.0 107.2 %all-gather.12.cloned.1.call-start = ((), (), s32[]{:S(2)}) async-start(), calls=%async_computation.6 | async-start | bytes 4718592 | tf_op jit(solution)/shard_map/all_gather | solution.py:40
  356.6 121.5 %all-reduce.15.cloned.1.call-start = ((), (), s32[]{:S(2)}) async-start(), calls=%async_computation.9 | async-start | bytes 2097152 | tf_op jit(solution)/shard_map/psum | solution.py:76
  357.3 5.8 slice-start
  358.6 4.6 slice-start.1
  371.9 106.2 %copy-start.5 = (f32[1024,128]{1,0:T(8,128)S(1)}, f32[1024,128]{1,0:T(8,128)}, u32[]{:S(2)}) copy-start(f32[1024,128]{1,0:T(8,128)} %param.14) | copy-start | bytes 1572868
  443.5 111.4 %all-gather.14.cloned.1.call-start = ((), (), s32[]{:S(2)}) async-start(), calls=%async_computation.7 | async-start | bytes 4718592 | tf_op jit(solution)/shard_map/all_gather | solution.py:40
  480.2 119.7 %all-reduce.13.cloned.1.call-start = ((), (), s32[]{:S(2)}) async-start(), calls=%async_computation.8 | async-start | bytes 1048576 | tf_op jit(solution)/shard_map/psum | solution.py:46
  480.2 88.1 %copy-start.2 = (f32[4,256,128]{1,2,0:T(8,128)S(1)}, f32[4,256,128]{1,2,0:T(8,128)}, u32[]{:S(2)}) copy-start(f32[4,256,128]{1,2,0:T(8,128)} %all-reduce.7.cloned.1.call-done) | copy-start | bytes 1572868
  480.2 89.1 %copy-start.3 = (f32[2,512,128]{1,2,0:T(8,128)S(1)}, f32[2,512,128]{1,2,0:T(8,128)}, u32[]{:S(2)}) copy-start(f32[2,512,128]{1,2,0:T(8,128)} %all-reduce.11.cloned.1.call-done) | copy-start | bytes 1572868
  554.8 47.1 %copy-start.1 = (f32[4,256,512]{2,1,0:T(8,128)S(1)}, f32[4,256,512]{2,1,0:T(8,128)}, u32[]{:S(2)}) copy-start(f32[4,256,512]{2,1,0:T(8,128)} %param.15) | copy-start | bytes 6291460
Sparse Core Ops, SparseCore 0:
  10.6 77.7 all-gather.5
  92.8 31.3 all-reduce.6
  126.2 75.0 all-gather.7
  209.9 31.3 all-reduce.8
  243.9 73.3 all-gather.9
  325.1 31.4 all-reduce.10
  358.8 73.3 all-gather.11
  443.6 34.4 all-reduce.14
  481.0 73.8 all-gather.13
  568.4 31.4 all-reduce.12
where the time goes:
time: 609 us
  waiting for transfers between devices  520 us (85%)
  matrix products  61.8 us (10%)
  between operations  14.4 us (2%)
  local copies, waits for them, and re-layouts  7.45 us (1%)
    all_gather x5, waiting for transfers between devices, fetch_columns(): gathered = lax.all_gather(block, 'rows', axis=1, tiled=True)  362 us
    psum x3, waiting for transfers between devices, solve_block(): solved = lax.psum(partial_value, 'cols')  92.6 us
    dot_general x6, matrix products, product(): jnp.einsum('src,sck->srk', matrix, vector, precision=lax.Precision.HIGHES...  52.8 us
    psum x1, waiting for transfers between devices, body(): resid_root = right_root[None] - root_summed - lax.psum(root_more, 'cols')  34.5 us
    psum x1, waiting for transfers between devices, body(): mid_summed, root_summed = lax.psum((mid_part, root_part), 'cols')  31.2 us
  transfers between devices with their start and end apart: 10, of which 10 were waited for; matrix products, arithmetic and copies ran while one was open for 3% of the time, Pallas kernels for 0%

commit v1 on v0

--- a/solution.py
+++ b/solution.py
@@ -37,7 +37,12 @@
 
 
 def fetch_columns(block):
-    gathered = lax.all_gather(block, "rows", axis=1, tiled=True)
+    ring = [block]
+    for hop in range(7):
+        ring.append(lax.ppermute(ring[-1], "rows", [(dev, (dev + 1) % 8) for dev in range(8)]))
+    gathered = jnp.roll(
+        jnp.concatenate(ring[::-1], axis=1), (lax.axis_index("rows") + 1) * ring[0].shape[1], axis=1
+    )
     return own_columns(gathered)
 
 

time: 609 us -> 725 us (1.19); the launches traced: 609 us -> 716 us
  waiting for transfers between devices: 520 us -> 609 us
  local copies, waits for them, and re-layouts: 7.45 us -> 35.9 us
  matrix products: 61.8 us -> 43.7 us
  starting transfers between devices: 0.59 us -> 10.1 us
    ppermute x0 -> x35, waiting for transfers between devices: none -> 453 us  [fetch_columns(): lax.ppermute(ring[-1], 'rows', [(dev, (dev + 1) % 8) for dev in range(8)])]
    all_gather x5 -> x0, waiting for transfers between devices: 362 us -> none  [fetch_columns(): gathered = lax.all_gather(block, 'rows', axis=1, tiled=True)]
    unnamed x27 -> x112, local copies, waits for them, and re-layouts: 6.46 us -> 34.7 us
    dot_general x6, matrix products: 52.8 us -> 39.9 us  [product(): jnp.einsum('src,sck->srk', matrix, vector, precision=lax.Precision.HIGHES...]
    ppermute x0 -> x35, starting transfers between devices: none -> 9.94 us  [fetch_columns(): lax.ppermute(ring[-1], 'rows', [(dev, (dev + 1) % 8) for dev in range(8)])]
  transfers between devices with their start and end apart: 10 -> 40, of which waited for: 10 -> 40; matrix products, arithmetic and copies ran while one was open for 3% -> 2% of each run, Pallas kernels for 0% -> 0%
where the time goes in v1:
time: 725 us; the launch traced here: 716 us
  waiting for transfers between devices  609 us (84%)
  matrix products  43.7 us (6%)
  local copies, waits for them, and re-layouts  35.9 us (5%)
  between operations  14.8 us (2%)
  starting transfers between devices  10.1 us (1%)
    ppermute x35, waiting for transfers between devices, fetch_columns(): lax.ppermute(ring[-1], 'rows', [(dev, (dev + 1) % 8) for dev in range(8)])  453 us
    psum x3, waiting for transfers between devices, solve_block(): solved = lax.psum(partial_value, 'cols')  89.5 us
    dot_general x6, matrix products, product(): jnp.einsum('src,sck->srk', matrix, vector, precision=lax.Precision.HIGHES...  39.9 us
    psum x1, waiting for transfers between devices, body(): resid_root = right_root[None] - root_summed - lax.psum(root_more, 'cols')  35.9 us
    unnamed x112, local copies, waits for them, and re-layouts  34.7 us
    psum x1, waiting for transfers between devices, body(): mid_summed, root_summed = lax.psum((mid_part, root_part), 'cols')  30.5 us
  transfers between devices with their start and end apart: 40, of which 40 were waited for; matrix products, arithmetic and copies ran while one was open for 2% of the time, Pallas kernels for 0%

profile of v1, /device:TPU:0, one launch (start us, length us, event | category | flops | bytes accessed | tf_op | source)
XLA Modules:
  0.0 716.4 jit_solution(5162113084156501975)
XLA Ops:
  8.6 3.0 collective-permute-start
  11.6 15.0 %collective-permute-done = f32[4,256,128]{1,2,0:T(8,128)S(1)} collective-permute-done((f32[4,256,128]{1,2,0:T(8,128)S(1)}, f32[4,256,128]{1,2,0:T(8,128)S(1)}, u32[]{:S(2)}, u32[]{:S(2)}) %collective-permute-start) | collective-permute-done | bytes 524320 | tf_op jit(solution)/shard_map/ppermute | solution.py:42
  26.6 15.8 %collective-permute-done.1 = f32[4,256,128]{1,2,0:T(8,128)S(1)} collective-permute-done((f32[4,256,128]{1,2,0:T(8,128)S(1)}, f32[4,256,128]{1,2,0:T(8,128)S(1)}, u32[]{:S(2)}, u32[]{:S(2)}) %collective-permute-start.1) | collective-permute-done | bytes 524320 | tf_op jit(solution)/shard_map/ppermute | solution.py:42
  43.2 14.9 %collective-permute-done.2 = f32[4,256,128]{1,2,0:T(8,128)S(1)} collective-permute-done((f32[4,256,128]{1,2,0:T(8,128)S(1)}, f32[4,256,128]{1,2,0:T(8,128)S(1)}, u32[]{:S(2)}, u32[]{:S(2)}) %collective-permute-start.2) | collective-permute-done | bytes 524320 | tf_op jit(solution)/shard_map/ppermute | solution.py:42
  58.9 14.0 %collective-permute-done.3 = f32[4,256,128]{1,2,0:T(8,128)S(1)} collective-permute-done((f32[4,256,128]{1,2,0:T(8,128)S(1)}, f32[4,256,128]{1,2,0:T(8,128)S(1)}, u32[]{:S(2)}, u32[]{:S(2)}) %collective-permute-start.3) | collective-permute-done | bytes 524320 | tf_op jit(solution)/shard_map/ppermute | solution.py:42
  73.6 13.0 %collective-permute-done.4 = f32[4,256,128]{1,2,0:T(8,128)S(1)} collective-permute-done((f32[4,256,128]{1,2,0:T(8,128)S(1)}, f32[4,256,128]{1,2,0:T(8,128)S(1)}, u32[]{:S(2)}, u32[]{:S(2)}) %collective-permute-start.4) | collective-permute-done | bytes 524320 | tf_op jit(solution)/shard_map/ppermute | solution.py:42
  87.5 12.2 %collective-permute-done.5 = f32[4,256,128]{1,2,0:T(8,128)} collective-permute-done((f32[4,256,128]{1,2,0:T(8,128)S(1)}, f32[4,256,128]{1,2,0:T(8,128)}, u32[]{:S(2)}, u32[]{:S(2)}) %collective-permute-start.5) | collective-permute-done | bytes 524320 | tf_op jit(solution)/shard_map/ppermute | solution.py:42
  99.7 12.2 %collective-permute-done.6 = f32[4,256,128]{1,2,0:T(8,128)} collective-permute-done((f32[4,256,128]{1,2,0:T(8,128)}, f32[4,256,128]{1,2,0:T(8,128)}, u32[]{:S(2)}, u32[]{:S(2)}) %collective-permute-start.6) | collective-permute-done | bytes 524320 | tf_op jit(solution)/shard_map/ppermute | solution.py:42
  116.7 3.2 convolution_bitcast_fusion.1
  120.0 30.4 %all-reduce.7.cloned.1.call-done = f32[4,256,128]{1,2,0:T(8,128)} async-done(((f32[4,256,128]{1,2,0:T(8,128)}), f32[4,256,128]{1,2,0:T(8,128)}) %all-reduce.7.cloned.1.call-update) | async-done | bytes 524304 | tf_op jit(solution)/shard_map/psum | solution.py:51
  151.9 14.0 %collective-permute-done.7 = f32[4,256,128]{1,2,0:T(8,128)S(1)} collective-permute-done((f32[4,256,128]{1,2,0:T(8,128)}, f32[4,256,128]{1,2,0:T(8,128)S(1)}, u32[]{:S(2)}, u32[]{:S(2)}) %collective-permute-start.7) | collective-permute-done | bytes 524320 | tf_op jit(solution)/shard_map/ppermute | solution.py:42
  165.8 14.3 %collective-permute-done.8 = f32[4,256,128]{1,2,0:T(8,128)S(1)} collective-permute-done((f32[4,256,128]{1,2,0:T(8,128)S(1)}, f32[4,256,128]{1,2,0:T(8,128)S(1)}, u32[]{:S(2)}, u32[]{:S(2)}) %collective-permute-start.8) | collective-permute-done | bytes 524320 | tf_op jit(solution)/shard_map/ppermute | solution.py:42
  180.1 13.4 %collective-permute-done.9 = f32[4,256,128]{1,2,0:T(8,128)S(1)} collective-permute-done((f32[4,256,128]{1,2,0:T(8,128)S(1)}, f32[4,256,128]{1,2,0:T(8,128)S(1)}, u32[]{:S(2)}, u32[]{:S(2)}) %collective-permute-start.9) | collective-permute-done | bytes 524320 | tf_op jit(solution)/shard_map/ppermute | solution.py:42
  193.5 12.5 %collective-permute-done.10 = f32[4,256,128]{1,2,0:T(8,128)S(1)} collective-permute-done((f32[4,256,128]{1,2,0:T(8,128)S(1)}, f32[4,256,128]{1,2,0:T(8,128)S(1)}, u32[]{:S(2)}, u32[]{:S(2)}) %collective-permute-start.10) | collective-permute-done | bytes 524320 | tf_op jit(solution)/shard_map/ppermute | solution.py:42
  206.0 12.6 %collective-permute-done.11 = f32[4,256,128]{1,2,0:T(8,128)S(1)} collective-permute-done((f32[4,256,128]{1,2,0:T(8,128)S(1)}, f32[4,256,128]{1,2,0:T(8,128)S(1)}, u32[]{:S(2)}, u32[]{:S(2)}) %collective-permute-start.11) | collective-permute-done | bytes 524320 | tf_op jit(solution)/shard_map/ppermute | solution.py:42
  218.7 13.5 %collective-permute-done.12 = f32[4,256,128]{1,2,0:T(8,128)} collective-permute-done((f32[4,256,128]{1,2,0:T(8,128)S(1)}, f32[4,256,128]{1,2,0:T(8,128)}, u32[]{:S(2)}, u32[]{:S(2)}) %collective-permute-start.12) | collective-permute-done | bytes 524320 | tf_op jit(solution)/shard_map/ppermute | solution.py:42
  233.1 11.2 %collective-permute-done.13 = f32[4,256,128]{1,2,0:T(8,128)S(1)} collective-permute-done((f32[4,256,128]{1,2,0:T(8,128)}, f32[4,256,128]{1,2,0:T(8,128)S(1)}, u32[]{:S(2)}, u32[]{:S(2)}) %collective-permute-start.13) | collective-permute-done | bytes 524320 | tf_op jit(solution)/shard_map/ppermute | solution.py:42
  248.9 4.1 bitcast_reduce_fusion
  254.3 30.5 %all-reduce.9.cloned.1.call-done = f32[2,512,128]{1,2,0:T(8,128)} async-done(((f32[2,512,128]{1,2,0:T(8,128)}), f32[2,512,128]{1,2,0:T(8,128)}) %all-reduce.9.cloned.1.call-update) | async-done | bytes 524304 | tf_op jit(solution)/shard_map/psum | solution.py:77
  287.4 13.8 %collective-permute-done.14 = f32[2,512,128]{1,2,0:T(8,128)S(1)} collective-permute-done((f32[2,512,128]{1,2,0:T(8,128)S(1)}, f32[2,512,128]{1,2,0:T(8,128)S(1)}, u32[]{:S(2)}, u32[]{:S(2)}) %collective-permute-start.14) | collective-permute-done | bytes 524320 | tf_op jit(solution)/shard_map/ppermute | solution.py:42
  301.2 14.3 %collective-permute-done.15 = f32[2,512,128]{1,2,0:T(8,128)S(1)} collective-permute-done((f32[2,512,128]{1,2,0:T(8,128)S(1)}, f32[2,512,128]{1,2,0:T(8,128)S(1)}, u32[]{:S(2)}, u32[]{:S(2)}) %collective-permute-start.15) | collective-permute-done | bytes 524320 | tf_op jit(solution)/shard_map/ppermute | solution.py:42
  315.5 13.4 %collective-permute-done.16 = f32[2,512,128]{1,2,0:T(8,128)S(1)} collective-permute-done((f32[2,512,128]{1,2,0:T(8,128)S(1)}, f32[2,512,128]{1,2,0:T(8,128)S(1)}, u32[]{:S(2)}, u32[]{:S(2)}) %collective-permute-start.16) | collective-permute-done | bytes 524320 | tf_op jit(solution)/shard_map/ppermute | solution.py:42
  328.9 12.5 %collective-permute-done.17 = f32[2,512,128]{1,2,0:T(8,128)S(1)} collective-permute-done((f32[2,512,128]{1,2,0:T(8,128)S(1)}, f32[2,512,128]{1,2,0:T(8,128)S(1)}, u32[]{:S(2)}, u32[]{:S(2)}) %collective-permute-start.17) | collective-permute-done | bytes 524320 | tf_op jit(solution)/shard_map/ppermute | solution.py:42
  341.3 11.9 %collective-permute-done.18 = f32[2,512,128]{1,2,0:T(8,128)S(1)} collective-permute-done((f32[2,512,128]{1,2,0:T(8,128)S(1)}, f32[2,512,128]{1,2,0:T(8,128)S(1)}, u32[]{:S(2)}, u32[]{:S(2)}) %collective-permute-start.18) | collective-permute-done | bytes 524320 | tf_op jit(solution)/shard_map/ppermute | solution.py:42
  354.0 13.1 %collective-permute-done.19 = f32[2,512,128]{1,2,0:T(8,128)} collective-permute-done((f32[2,512,128]{1,2,0:T(8,128)S(1)}, f32[2,512,128]{1,2,0:T(8,128)}, u32[]{:S(2)}, u32[]{:S(2)}) %collective-permute-start.19) | collective-permute-done | bytes 524320 | tf_op jit(solution)/shard_map/ppermute | solution.py:42
  367.6 12.1 %collective-permute-done.20 = f32[2,512,128]{1,2,0:T(8,128)} collective-permute-done((f32[2,512,128]{1,2,0:T(8,128)}, f32[2,512,128]{1,2,0:T(8,128)}, u32[]{:S(2)}, u32[]{:S(2)}) %collective-permute-start.20) | collective-permute-done | bytes 524320 | tf_op jit(solution)/shard_map/ppermute | solution.py:42
  383.3 5.1 convolution_bitcast_fusion.2
  388.4 31.4 %all-reduce.11.cloned.1.call-done = f32[2,512,128]{1,2,0:T(8,128)} async-done(((f32[2,512,128]{1,2,0:T(8,128)}), f32[2,512,128]{1,2,0:T(8,128)}) %all-reduce.11.cloned.1.call-update) | async-done | bytes 524304 | tf_op jit(solution)/shard_map/psum | solution.py:51
  421.3 14.0 %collective-permute-done.21 = f32[2,512,128]{1,2,0:T(8,128)S(1)} collective-permute-done((f32[2,512,128]{1,2,0:T(8,128)}, f32[2,512,128]{1,2,0:T(8,128)S(1)}, u32[]{:S(2)}, u32[]{:S(2)}) %collective-permute-start.21) | collective-permute-done | bytes 524320 | tf_op jit(solution)/shard_map/ppermute | solution.py:42
  435.3 14.3 %collective-permute-done.22 = f32[2,512,128]{1,2,0:T(8,128)S(1)} collective-permute-done((f32[2,512,128]{1,2,0:T(8,128)S(1)}, f32[2,512,128]{1,2,0:T(8,128)S(1)}, u32[]{:S(2)}, u32[]{:S(2)}) %collective-permute-start.22) | collective-permute-done | bytes 524320 | tf_op jit(solution)/shard_map/ppermute | solution.py:42
  449.6 13.4 %collective-permute-done.23 = f32[2,512,128]{1,2,0:T(8,128)S(1)} collective-permute-done((f32[2,512,128]{1,2,0:T(8,128)S(1)}, f32[2,512,128]{1,2,0:T(8,128)S(1)}, u32[]{:S(2)}, u32[]{:S(2)}) %collective-permute-start.23) | collective-permute-done | bytes 524320 | tf_op jit(solution)/shard_map/ppermute | solution.py:42
  463.2 12.2 %collective-permute-done.24 = f32[2,512,128]{1,2,0:T(8,128)S(1)} collective-permute-done((f32[2,512,128]{1,2,0:T(8,128)S(1)}, f32[2,512,128]{1,2,0:T(8,128)S(1)}, u32[]{:S(2)}, u32[]{:S(2)}) %collective-permute-start.24) | collective-permute-done | bytes 524320 | tf_op jit(solution)/shard_map/ppermute | solution.py:42
  476.9 11.2 %collective-permute-done.25 = f32[2,512,128]{1,2,0:T(8,128)S(1)} collective-permute-done((f32[2,512,128]{1,2,0:T(8,128)S(1)}, f32[2,512,128]{1,2,0:T(8,128)S(1)}, u32[]{:S(2)}, u32[]{:S(2)}) %collective-permute-start.25) | collective-permute-done | bytes 524320 | tf_op jit(solution)/shard_map/ppermute | solution.py:42
  489.5 12.0 %collective-permute-done.26 = f32[2,512,128]{1,2,0:T(8,128)} collective-permute-done((f32[2,512,128]{1,2,0:T(8,128)S(1)}, f32[2,512,128]{1,2,0:T(8,128)}, u32[]{:S(2)}, u32[]{:S(2)}) %collective-permute-start.26) | collective-permute-done | bytes 524320 | tf_op jit(solution)/shard_map/ppermute | solution.py:42
  501.7 10.2 %fusion.6 = f32[1,1024,128]{2,1,0:T(8,128)} fusion(f32[4,1024,512]{2,1,0:T(8,128)} %param.23, f32[4,1024,512]{2,1,0:T(8,128)S(1)} %fusion.33, s32[]{:T(128)S(6)} %add.152, f32[4,2048,128]{1,2,0:T(8,128)S(1)} %copy-done.3), kind=kOutput, calls=%fused_computation.14 | convolution fusion | flops 3223584768 | bytes 21495812 | tf_op jit(solution)/shard_map/src,sck->srk/dot_general | solution.py:10
  511.8 2.0 collective-permute-done.27
  517.3 7.6 %fusion.9 = f32[1,1024,128]{2,1,0:T(8,128)} fusion(f32[2,1024,1024]{2,1,0:T(8,128)S(1)} %bitcast.58, f32[2,1024,1024]{2,1,0:T(8,128)S(1)} %fusion.27, s32[]{:T(128)S(6)} %add.158, f32[2,4096,128]{1,2,0:T(8,128)S(1)} %constant_dynamic-update-slice_fusion.24), kind=kOutput, calls=%fused_computation.15 | convolution fusion | flops 3223584768 | bytes 21495812 | tf_op jit(solution)/shard_map/src,sck->srk/dot_general | solution.py:10
  525.0 35.9 %all-reduce.15.cloned.1.call-done = (f32[1,1024,128]{2,1,0:T(8,128)}, f32[1,1024,128]{2,1,0:T(8,128)}) async-done(((f32[1,1024,128]{2,1,0:T(8,128)}, f32[1,1024,128]{2,1,0:T(8,128)}), (f32[1,1024,128]{2,1,0:T(8,128)}, f32[1,1024,128]{2,1,0:T(8,128)})) %all-reduce.15.cloned.1.call-update) | async-done | bytes 1048592 | tf_op jit(solution)/shard_map/psum | solution.py:81
  563.7 14.7 %collective-permute-done.28 = f32[1,1024,128]{2,1,0:T(8,128)S(1)} collective-permute-done((f32[1,1024,128]{2,1,0:T(8,128)S(1)}, f32[1,1024,128]{2,1,0:T(8,128)S(1)}, u32[]{:S(2)}, u32[]{:S(2)}) %collective-permute-start.28) | collective-permute-done | bytes 524320 | tf_op jit(solution)/shard_map/ppermute | solution.py:42
  578.4 15.3 %collective-permute-done.29 = f32[1,1024,128]{2,1,0:T(8,128)S(1)} collective-permute-done((f32[1,1024,128]{2,1,0:T(8,128)S(1)}, f32[1,1024,128]{2,1,0:T(8,128)S(1)}, u32[]{:S(2)}, u32[]{:S(2)}) %collective-permute-start.29) | collective-permute-done | bytes 524320 | tf_op jit(solution)/shard_map/ppermute | solution.py:42
  593.7 14.4 %collective-permute-done.30 = f32[1,1024,128]{2,1,0:T(8,128)S(1)} collective-permute-done((f32[1,1024,128]{2,1,0:T(8,128)S(1)}, f32[1,1024,128]{2,1,0:T(8,128)S(1)}, u32[]{:S(2)}, u32[]{:S(2)}) %collective-permute-start.30) | collective-permute-done | bytes 524320 | tf_op jit(solution)/shard_map/ppermute | solution.py:42
  608.1 13.4 %collective-permute-done.31 = f32[1,1024,128]{2,1,0:T(8,128)S(1)} collective-permute-done((f32[1,1024,128]{2,1,0:T(8,128)S(1)}, f32[1,1024,128]{2,1,0:T(8,128)S(1)}, u32[]{:S(2)}, u32[]{:S(2)}) %collective-permute-start.31) | collective-permute-done | bytes 524320 | tf_op jit(solution)/shard_map/ppermute | solution.py:42
  622.3 12.5 %collective-permute-done.32 = f32[1,1024,128]{2,1,0:T(8,128)S(1)} collective-permute-done((f32[1,1024,128]{2,1,0:T(8,128)S(1)}, f32[1,1024,128]{2,1,0:T(8,128)S(1)}, u32[]{:S(2)}, u32[]{:S(2)}) %collective-permute-start.32) | collective-permute-done | bytes 524320 | tf_op jit(solution)/shard_map/ppermute | solution.py:42
  635.9 12.4 %collective-permute-done.33 = f32[1,1024,128]{2,1,0:T(8,128)} collective-permute-done((f32[1,1024,128]{2,1,0:T(8,128)S(1)}, f32[1,1024,128]{2,1,0:T(8,128)}, u32[]{:S(2)}, u32[]{:S(2)}) %collective-permute-start.33) | collective-permute-done | bytes 524320 | tf_op jit(solution)/shard_map/ppermute | solution.py:42
  648.3 12.2 %collective-permute-done.34 = f32[1,1024,128]{2,1,0:T(8,128)} collective-permute-done((f32[1,1024,128]{2,1,0:T(8,128)}, f32[1,1024,128]{2,1,0:T(8,128)}, u32[]{:S(2)}, u32[]{:S(2)}) %collective-permute-start.34) | collective-permute-done | bytes 524320 | tf_op jit(solution)/shard_map/ppermute | solution.py:42
  668.2 9.6 %convolution_bitcast_fusion = f32[1024,128]{0,1:T(8,128)} fusion(f32[1024,2048]{1,0:T(8,128)S(1)} %bitcast.56, f32[1,16384,128]{2,1,0:T(8,128)S(1)} %constant_dynamic-update-slice_fusion.32, s32[]{:T(128)S(6)} %dynamic_slice.30), kind=kOutput, calls=%fused_computation.16 | convolution fusion | flops 3221225472 | bytes 9961476 | tf_op jit(solution)/shard_map/src,sck->srk/dot_general | solution.py:10
  679.9 27.7 %all-reduce.13.cloned.1.call-done = f32[1024,128]{0,1:T(8,128)} async-done(((f32[1024,128]{0,1:T(8,128)}), f32[1024,128]{0,1:T(8,128)}) %all-reduce.13.cloned.1.call-update) | async-done | bytes 524304 | tf_op jit(solution)/shard_map/psum | solution.py:51
  707.6 2.0 copy.43
  (178 shorter events, 47.3 us)
Async XLA Ops:
  7.2 109.5 %copy-start = (f32[4,256,512]{2,1,0:T(8,128)S(1)}, f32[4,256,512]{2,1,0:T(8,128)}, u32[]{:S(2)}) copy-start(f32[4,256,512]{2,1,0:T(8,128)} %param.19) | copy-start | bytes 6291460
  7.2 143.2 %all-reduce.7.cloned.1.call-start = ((), (), s32[]{:S(2)}) async-start(), calls=%async_computation | async-start | bytes 1048576 | tf_op jit(solution)/shard_map/psum | solution.py:51
  8.6 18.0 %collective-permute-start = (f32[4,256,128]{1,2,0:T(8,128)S(1)}, f32[4,256,128]{1,2,0:T(8,128)S(1)}, u32[]{:S(2)}, u32[]{:S(2)}) collective-permute-start(f32[4,256,128]{1,2,0:T(8,128)S(1)} %copy.34), channel_id=1, source_target_pairs={{0,4},{4,8},{8,12},{12,16},{16,20},{20,24},{24,28},{28,0},{1,5},{5... | collective-permute-start | bytes 1572872 | tf_op jit(solution)/shard_map/ppermute | solution.py:42
  26.6 15.8 %collective-permute-start.1 = (f32[4,256,128]{1,2,0:T(8,128)S(1)}, f32[4,256,128]{1,2,0:T(8,128)S(1)}, u32[]{:S(2)}, u32[]{:S(2)}) collective-permute-start(f32[4,256,128]{1,2,0:T(8,128)S(1)} %collective-permute-done), channel_id=1, source_target_pairs={{0,4},{4,8},{8,12},{12,16},{16,20},{20,24},{24,28},{28,0},{1,5},{5... | collective-permute-start | bytes 1572872 | tf_op jit(solution)/shard_map/ppermute | solution.py:42
  43.2 14.9 %collective-permute-start.2 = (f32[4,256,128]{1,2,0:T(8,128)S(1)}, f32[4,256,128]{1,2,0:T(8,128)S(1)}, u32[]{:S(2)}, u32[]{:S(2)}) collective-permute-start(f32[4,256,128]{1,2,0:T(8,128)S(1)} %collective-permute-done.1), channel_id=1, source_target_pairs={{0,4},{4,8},{8,12},{12,16},{16,20},{20,24},{24,28},{28,0},{1,5},{5... | collective-permute-start | bytes 1572872 | tf_op jit(solution)/shard_map/ppermute | solution.py:42
  58.9 14.0 %collective-permute-start.3 = (f32[4,256,128]{1,2,0:T(8,128)S(1)}, f32[4,256,128]{1,2,0:T(8,128)S(1)}, u32[]{:S(2)}, u32[]{:S(2)}) collective-permute-start(f32[4,256,128]{1,2,0:T(8,128)S(1)} %collective-permute-done.2), channel_id=1, source_target_pairs={{0,4},{4,8},{8,12},{12,16},{16,20},{20,24},{24,28},{28,0},{1,5},{5... | collective-permute-start | bytes 1572872 | tf_op jit(solution)/shard_map/ppermute | solution.py:42
  73.6 13.0 %collective-permute-start.4 = (f32[4,256,128]{1,2,0:T(8,128)S(1)}, f32[4,256,128]{1,2,0:T(8,128)S(1)}, u32[]{:S(2)}, u32[]{:S(2)}) collective-permute-start(f32[4,256,128]{1,2,0:T(8,128)S(1)} %collective-permute-done.3), channel_id=1, source_target_pairs={{0,4},{4,8},{8,12},{12,16},{16,20},{20,24},{24,28},{28,0},{1,5},{5... | collective-permute-start | bytes 1572872 | tf_op jit(solution)/shard_map/ppermute | solution.py:42
  87.5 12.2 %collective-permute-start.5 = (f32[4,256,128]{1,2,0:T(8,128)S(1)}, f32[4,256,128]{1,2,0:T(8,128)}, u32[]{:S(2)}, u32[]{:S(2)}) collective-permute-start(f32[4,256,128]{1,2,0:T(8,128)S(1)} %collective-permute-done.4), channel_id=1, source_target_pairs={{0,4},{4,8},{8,12},{12,16},{16,20},{20,24},{24,28},{28,0},{1,5},{5... | collective-permute-start | bytes 1572872 | tf_op jit(solution)/shard_map/ppermute | solution.py:42
  99.7 12.2 %collective-permute-start.6 = (f32[4,256,128]{1,2,0:T(8,128)}, f32[4,256,128]{1,2,0:T(8,128)}, u32[]{:S(2)}, u32[]{:S(2)}) collective-permute-start(f32[4,256,128]{1,2,0:T(8,128)} %collective-permute-done.5), channel_id=1, source_target_pairs={{0,4},{4,8},{8,12},{12,16},{16,20},{20,24},{24,28},{28,0},{1,5},{5... | collective-permute-start | bytes 1572872 | tf_op jit(solution)/shard_map/ppermute | solution.py:42
  116.6 102.1 %copy-start.25 = (s32[4,32,16]{1,2,0:T(8,128)S(1)}, s32[4,32,16]{1,2,0:T(8,128)}, u32[]{:S(2)}) copy-start(s32[4,32,16]{1,2,0:T(8,128)} %param.25) | copy-start | bytes 24580
  119.9 164.8 %all-reduce.9.cloned.1.call-start = ((), (), s32[]{:S(2)}) async-start(), calls=%async_computation.1 | async-start | bytes 1048576 | tf_op jit(solution)/shard_map/psum | solution.py:77
  150.4 15.4 %collective-permute-start.7 = (f32[4,256,128]{1,2,0:T(8,128)}, f32[4,256,128]{1,2,0:T(8,128)S(1)}, u32[]{:S(2)}, u32[]{:S(2)}) collective-permute-start(f32[4,256,128]{1,2,0:T(8,128)} %all-reduce.7.cloned.1.call-done), channel_id=1, source_target_pairs={{0,4},{4,8},{8,12},{12,16},{16,20},{20,24},{24,28},{28,0},{1,5},{5... | collective-permute-start | bytes 1572872 | tf_op jit(solution)/shard_map/ppermute | solution.py:42
  165.8 14.3 %collective-permute-start.8 = (f32[4,256,128]{1,2,0:T(8,128)S(1)}, f32[4,256,128]{1,2,0:T(8,128)S(1)}, u32[]{:S(2)}, u32[]{:S(2)}) collective-permute-start(f32[4,256,128]{1,2,0:T(8,128)S(1)} %collective-permute-done.7), channel_id=1, source_target_pairs={{0,4},{4,8},{8,12},{12,16},{16,20},{20,24},{24,28},{28,0},{1,5},{5... | collective-permute-start | bytes 1572872 | tf_op jit(solution)/shard_map/ppermute | solution.py:42
  180.1 13.4 %collective-permute-start.9 = (f32[4,256,128]{1,2,0:T(8,128)S(1)}, f32[4,256,128]{1,2,0:T(8,128)S(1)}, u32[]{:S(2)}, u32[]{:S(2)}) collective-permute-start(f32[4,256,128]{1,2,0:T(8,128)S(1)} %collective-permute-done.8), channel_id=1, source_target_pairs={{0,4},{4,8},{8,12},{12,16},{16,20},{20,24},{24,28},{28,0},{1,5},{5... | collective-permute-start | bytes 1572872 | tf_op jit(solution)/shard_map/ppermute | solution.py:42
  193.5 12.5 %collective-permute-start.10 = (f32[4,256,128]{1,2,0:T(8,128)S(1)}, f32[4,256,128]{1,2,0:T(8,128)S(1)}, u32[]{:S(2)}, u32[]{:S(2)}) collective-permute-start(f32[4,256,128]{1,2,0:T(8,128)S(1)} %collective-permute-done.9), channel_id=1, source_target_pairs={{0,4},{4,8},{8,12},{12,16},{16,20},{20,24},{24,28},{28,0},{1,5},{5... | collective-permute-start | bytes 1572872 | tf_op jit(solution)/shard_map/ppermute | solution.py:42
  206.0 12.6 %collective-permute-start.11 = (f32[4,256,128]{1,2,0:T(8,128)S(1)}, f32[4,256,128]{1,2,0:T(8,128)S(1)}, u32[]{:S(2)}, u32[]{:S(2)}) collective-permute-start(f32[4,256,128]{1,2,0:T(8,128)S(1)} %collective-permute-done.10), channel_id=1, source_target_pairs={{0,4},{4,8},{8,12},{12,16},{16,20},{20,24},{24,28},{28,0},{1,5},{5... | collective-permute-start | bytes 1572872 | tf_op jit(solution)/shard_map/ppermute | solution.py:42
  218.6 13.5 %collective-permute-start.12 = (f32[4,256,128]{1,2,0:T(8,128)S(1)}, f32[4,256,128]{1,2,0:T(8,128)}, u32[]{:S(2)}, u32[]{:S(2)}) collective-permute-start(f32[4,256,128]{1,2,0:T(8,128)S(1)} %collective-permute-done.11), channel_id=1, source_target_pairs={{0,4},{4,8},{8,12},{12,16},{16,20},{20,24},{24,28},{28,0},{1,5},{5... | collective-permute-start | bytes 1572872 | tf_op jit(solution)/shard_map/ppermute | solution.py:42
  232.2 12.1 %collective-permute-start.13 = (f32[4,256,128]{1,2,0:T(8,128)}, f32[4,256,128]{1,2,0:T(8,128)S(1)}, u32[]{:S(2)}, u32[]{:S(2)}) collective-permute-start(f32[4,256,128]{1,2,0:T(8,128)} %collective-permute-done.12), channel_id=1, source_target_pairs={{0,4},{4,8},{8,12},{12,16},{16,20},{20,24},{24,28},{28,0},{1,5},{5... | collective-permute-start | bytes 1572872 | tf_op jit(solution)/shard_map/ppermute | solution.py:42
  254.0 165.8 %all-reduce.11.cloned.1.call-start = ((), (), s32[]{:S(2)}) async-start(), calls=%async_computation.2 | async-start | bytes 1048576 | tf_op jit(solution)/shard_map/psum | solution.py:51
  285.9 15.3 %collective-permute-start.14 = (f32[2,512,128]{1,2,0:T(8,128)S(1)}, f32[2,512,128]{1,2,0:T(8,128)S(1)}, u32[]{:S(2)}, u32[]{:S(2)}) collective-permute-start(f32[2,512,128]{1,2,0:T(8,128)S(1)} %sub.45), channel_id=1, source_target_pairs={{0,4},{4,8},{8,12},{12,16},{16,20},{20,24},{24,28},{28,0},{1,5},{5... | collective-permute-start | bytes 1572872 | tf_op jit(solution)/shard_map/ppermute | solution.py:42
  301.2 14.3 %collective-permute-start.15 = (f32[2,512,128]{1,2,0:T(8,128)S(1)}, f32[2,512,128]{1,2,0:T(8,128)S(1)}, u32[]{:S(2)}, u32[]{:S(2)}) collective-permute-start(f32[2,512,128]{1,2,0:T(8,128)S(1)} %collective-permute-done.14), channel_id=1, source_target_pairs={{0,4},{4,8},{8,12},{12,16},{16,20},{20,24},{24,28},{28,0},{1,5},{5... | collective-permute-start | bytes 1572872 | tf_op jit(solution)/shard_map/ppermute | solution.py:42
  315.5 13.4 %collective-permute-start.16 = (f32[2,512,128]{1,2,0:T(8,128)S(1)}, f32[2,512,128]{1,2,0:T(8,128)S(1)}, u32[]{:S(2)}, u32[]{:S(2)}) collective-permute-start(f32[2,512,128]{1,2,0:T(8,128)S(1)} %collective-permute-done.15), channel_id=1, source_target_pairs={{0,4},{4,8},{8,12},{12,16},{16,20},{20,24},{24,28},{28,0},{1,5},{5... | collective-permute-start | bytes 1572872 | tf_op jit(solution)/shard_map/ppermute | solution.py:42
  328.9 12.5 %collective-permute-start.17 = (f32[2,512,128]{1,2,0:T(8,128)S(1)}, f32[2,512,128]{1,2,0:T(8,128)S(1)}, u32[]{:S(2)}, u32[]{:S(2)}) collective-permute-start(f32[2,512,128]{1,2,0:T(8,128)S(1)} %collective-permute-done.16), channel_id=1, source_target_pairs={{0,4},{4,8},{8,12},{12,16},{16,20},{20,24},{24,28},{28,0},{1,5},{5... | collective-permute-start | bytes 1572872 | tf_op jit(solution)/shard_map/ppermute | solution.py:42
  341.3 11.9 %collective-permute-start.18 = (f32[2,512,128]{1,2,0:T(8,128)S(1)}, f32[2,512,128]{1,2,0:T(8,128)S(1)}, u32[]{:S(2)}, u32[]{:S(2)}) collective-permute-start(f32[2,512,128]{1,2,0:T(8,128)S(1)} %collective-permute-done.17), channel_id=1, source_target_pairs={{0,4},{4,8},{8,12},{12,16},{16,20},{20,24},{24,28},{28,0},{1,5},{5... | collective-permute-start | bytes 1572872 | tf_op jit(solution)/shard_map/ppermute | solution.py:42
  354.0 13.1 %collective-permute-start.19 = (f32[2,512,128]{1,2,0:T(8,128)S(1)}, f32[2,512,128]{1,2,0:T(8,128)}, u32[]{:S(2)}, u32[]{:S(2)}) collective-permute-start(f32[2,512,128]{1,2,0:T(8,128)S(1)} %collective-permute-done.18), channel_id=1, source_target_pairs={{0,4},{4,8},{8,12},{12,16},{16,20},{20,24},{24,28},{28,0},{1,5},{5... | collective-permute-start | bytes 1572872 | tf_op jit(solution)/shard_map/ppermute | solution.py:42
  367.1 12.6 %collective-permute-start.20 = (f32[2,512,128]{1,2,0:T(8,128)}, f32[2,512,128]{1,2,0:T(8,128)}, u32[]{:S(2)}, u32[]{:S(2)}) collective-permute-start(f32[2,512,128]{1,2,0:T(8,128)} %collective-permute-done.19), channel_id=1, source_target_pairs={{0,4},{4,8},{8,12},{12,16},{16,20},{20,24},{24,28},{28,0},{1,5},{5... | collective-permute-start | bytes 1572872 | tf_op jit(solution)/shard_map/ppermute | solution.py:42
  383.2 79.8 %copy-start.26 = (s32[4,64,16]{1,2,0:T(8,128)S(1)}, s32[4,64,16]{1,2,0:T(8,128)}, u32[]{:S(2)}) copy-start(s32[4,64,16]{1,2,0:T(8,128)} %param.26) | copy-start | bytes 49156
  383.3 79.8 %copy-start.27 = (s32[2,64,32]{1,2,0:T(8,128)S(1)}, s32[2,64,32]{1,2,0:T(8,128)}, u32[]{:S(2)}) copy-start(s32[2,64,32]{1,2,0:T(8,128)} %param.27) | copy-start | bytes 49156
  388.4 172.5 %all-reduce.15.cloned.1.call-start = ((), (), s32[]{:S(2)}) async-start(), calls=%async_computation.4 | async-start | bytes 2097152 | tf_op jit(solution)/shard_map/psum | solution.py:81
  419.9 15.4 %collective-permute-start.21 = (f32[2,512,128]{1,2,0:T(8,128)}, f32[2,512,128]{1,2,0:T(8,128)S(1)}, u32[]{:S(2)}, u32[]{:S(2)}) collective-permute-start(f32[2,512,128]{1,2,0:T(8,128)} %all-reduce.11.cloned.1.call-done), channel_id=1, source_target_pairs={{0,4},{4,8},{8,12},{12,16},{16,20},{20,24},{24,28},{28,0},{1,5},{5... | collective-permute-start | bytes 1572872 | tf_op jit(solution)/shard_map/ppermute | solution.py:42
  435.3 14.3 %collective-permute-start.22 = (f32[2,512,128]{1,2,0:T(8,128)S(1)}, f32[2,512,128]{1,2,0:T(8,128)S(1)}, u32[]{:S(2)}, u32[]{:S(2)}) collective-permute-start(f32[2,512,128]{1,2,0:T(8,128)S(1)} %collective-permute-done.21), channel_id=1, source_target_pairs={{0,4},{4,8},{8,12},{12,16},{16,20},{20,24},{24,28},{28,0},{1,5},{5... | collective-permute-start | bytes 1572872 | tf_op jit(solution)/shard_map/ppermute | solution.py:42
  449.6 13.4 %collective-permute-start.23 = (f32[2,512,128]{1,2,0:T(8,128)S(1)}, f32[2,512,128]{1,2,0:T(8,128)S(1)}, u32[]{:S(2)}, u32[]{:S(2)}) collective-permute-start(f32[2,512,128]{1,2,0:T(8,128)S(1)} %collective-permute-done.22), channel_id=1, source_target_pairs={{0,4},{4,8},{8,12},{12,16},{16,20},{20,24},{24,28},{28,0},{1,5},{5... | collective-permute-start | bytes 1572872 | tf_op jit(solution)/shard_map/ppermute | solution.py:42
  463.0 12.5 %collective-permute-start.24 = (f32[2,512,128]{1,2,0:T(8,128)S(1)}, f32[2,512,128]{1,2,0:T(8,128)S(1)}, u32[]{:S(2)}, u32[]{:S(2)}) collective-permute-start(f32[2,512,128]{1,2,0:T(8,128)S(1)} %collective-permute-done.23), channel_id=1, source_target_pairs={{0,4},{4,8},{8,12},{12,16},{16,20},{20,24},{24,28},{28,0},{1,5},{5... | collective-permute-start | bytes 1572872 | tf_op jit(solution)/shard_map/ppermute | solution.py:42
  475.5 12.6 %collective-permute-start.25 = (f32[2,512,128]{1,2,0:T(8,128)S(1)}, f32[2,512,128]{1,2,0:T(8,128)S(1)}, u32[]{:S(2)}, u32[]{:S(2)}) collective-permute-start(f32[2,512,128]{1,2,0:T(8,128)S(1)} %collective-permute-done.24), channel_id=1, source_target_pairs={{0,4},{4,8},{8,12},{12,16},{16,20},{20,24},{24,28},{28,0},{1,5},{5... | collective-permute-start | bytes 1572872 | tf_op jit(solution)/shard_map/ppermute | solution.py:42
  488.1 13.4 %collective-permute-start.26 = (f32[2,512,128]{1,2,0:T(8,128)S(1)}, f32[2,512,128]{1,2,0:T(8,128)}, u32[]{:S(2)}, u32[]{:S(2)}) collective-permute-start(f32[2,512,128]{1,2,0:T(8,128)S(1)} %collective-permute-done.25), channel_id=1, source_target_pairs={{0,4},{4,8},{8,12},{12,16},{16,20},{20,24},{24,28},{28,0},{1,5},{5... | collective-permute-start | bytes 1572872 | tf_op jit(solution)/shard_map/ppermute | solution.py:42
  488.1 29.2 %slice-start.2 = ((s8[8388608]{0:T(1024)(128)(4,1)}), s8[4194304]{0:T(1024)(128)(4,1)S(1)}, s32[]{:S(2)}) async-start(s8[8388608]{0:T(1024)(128)(4,1)} %bitcast.57), calls=%async_computation.7 | async-start | bytes 8388608
  489.4 27.9 %slice-start.3 = ((s8[8388608]{0:T(1024)(128)(4,1)}), s8[4194304]{0:T(1024)(128)(4,1)S(1)}, s32[]{:S(2)}) async-start(s8[8388608]{0:T(1024)(128)(4,1)} %bitcast.57), calls=%async_computation.8 | async-start | bytes 8388608
  501.5 12.3 %collective-permute-start.27 = (f32[2,512,128]{1,2,0:T(8,128)}, f32[2,512,128]{1,2,0:T(8,128)}, u32[]{:S(2)}, u32[]{:S(2)}) collective-permute-start(f32[2,512,128]{1,2,0:T(8,128)} %collective-permute-done.26), channel_id=1, source_target_pairs={{0,4},{4,8},{8,12},{12,16},{16,20},{20,24},{24,28},{28,0},{1,5},{5... | collective-permute-start | bytes 1572872 | tf_op jit(solution)/shard_map/ppermute | solution.py:42
  517.3 43.6 %copy-start.24 = (f32[1024,128]{1,0:T(8,128)S(1)}, f32[1024,128]{1,0:T(8,128)}, u32[]{:S(2)}) copy-start(f32[1024,128]{1,0:T(8,128)} %param.18) | copy-start | bytes 1572868
  525.0 182.6 %all-reduce.13.cloned.1.call-start = ((), (), s32[]{:S(2)}) async-start(), calls=%async_computation.3 | async-start | bytes 1048576 | tf_op jit(solution)/shard_map/psum | solution.py:51
  562.2 16.2 %collective-permute-start.28 = (f32[1,1024,128]{2,1,0:T(8,128)S(1)}, f32[1,1024,128]{2,1,0:T(8,128)S(1)}, u32[]{:S(2)}, u32[]{:S(2)}) collective-permute-start(f32[1,1024,128]{2,1,0:T(8,128)S(1)} %fusion.21), channel_id=1, source_target_pairs={{0,4},{4,8},{8,12},{12,16},{16,20},{20,24},{24,28},{28,0},{1,5},{5... | collective-permute-start | bytes 1572872 | tf_op jit(solution)/shard_map/ppermute | solution.py:42
  578.4 15.3 %collective-permute-start.29 = (f32[1,1024,128]{2,1,0:T(8,128)S(1)}, f32[1,1024,128]{2,1,0:T(8,128)S(1)}, u32[]{:S(2)}, u32[]{:S(2)}) collective-permute-start(f32[1,1024,128]{2,1,0:T(8,128)S(1)} %collective-permute-done.28), channel_id=1, source_target_pairs={{0,4},{4,8},{8,12},{12,16},{16,20},{20,24},{24,28},{28,0},{1,5},{5... | collective-permute-start | bytes 1572872 | tf_op jit(solution)/shard_map/ppermute | solution.py:42
  593.7 14.4 %collective-permute-start.30 = (f32[1,1024,128]{2,1,0:T(8,128)S(1)}, f32[1,1024,128]{2,1,0:T(8,128)S(1)}, u32[]{:S(2)}, u32[]{:S(2)}) collective-permute-start(f32[1,1024,128]{2,1,0:T(8,128)S(1)} %collective-permute-done.29), channel_id=1, source_target_pairs={{0,4},{4,8},{8,12},{12,16},{16,20},{20,24},{24,28},{28,0},{1,5},{5... | collective-permute-start | bytes 1572872 | tf_op jit(solution)/shard_map/ppermute | solution.py:42
  608.1 13.4 %collective-permute-start.31 = (f32[1,1024,128]{2,1,0:T(8,128)S(1)}, f32[1,1024,128]{2,1,0:T(8,128)S(1)}, u32[]{:S(2)}, u32[]{:S(2)}) collective-permute-start(f32[1,1024,128]{2,1,0:T(8,128)S(1)} %collective-permute-done.30), channel_id=1, source_target_pairs={{0,4},{4,8},{8,12},{12,16},{16,20},{20,24},{24,28},{28,0},{1,5},{5... | collective-permute-start | bytes 1572872 | tf_op jit(solution)/shard_map/ppermute | solution.py:42
  622.3 12.5 %collective-permute-start.32 = (f32[1,1024,128]{2,1,0:T(8,128)S(1)}, f32[1,1024,128]{2,1,0:T(8,128)S(1)}, u32[]{:S(2)}, u32[]{:S(2)}) collective-permute-start(f32[1,1024,128]{2,1,0:T(8,128)S(1)} %collective-permute-done.31), channel_id=1, source_target_pairs={{0,4},{4,8},{8,12},{12,16},{16,20},{20,24},{24,28},{28,0},{1,5},{5... | collective-permute-start | bytes 1572872 | tf_op jit(solution)/shard_map/ppermute | solution.py:42
  635.6 12.6 %collective-permute-start.33 = (f32[1,1024,128]{2,1,0:T(8,128)S(1)}, f32[1,1024,128]{2,1,0:T(8,128)}, u32[]{:S(2)}, u32[]{:S(2)}) collective-permute-start(f32[1,1024,128]{2,1,0:T(8,128)S(1)} %collective-permute-done.32), channel_id=1, source_target_pairs={{0,4},{4,8},{8,12},{12,16},{16,20},{20,24},{24,28},{28,0},{1,5},{5... | collective-permute-start | bytes 1572872 | tf_op jit(solution)/shard_map/ppermute | solution.py:42
  648.3 12.2 %collective-permute-start.34 = (f32[1,1024,128]{2,1,0:T(8,128)}, f32[1,1024,128]{2,1,0:T(8,128)}, u32[]{:S(2)}, u32[]{:S(2)}) collective-permute-start(f32[1,1024,128]{2,1,0:T(8,128)} %collective-permute-done.33), channel_id=1, source_target_pairs={{0,4},{4,8},{8,12},{12,16},{16,20},{20,24},{24,28},{28,0},{1,5},{5... | collective-permute-start | bytes 1572872 | tf_op jit(solution)/shard_map/ppermute | solution.py:42
  668.2 41.4 %copy-start.1 = (f32[4,256,512]{2,1,0:T(8,128)S(1)}, f32[4,256,512]{2,1,0:T(8,128)}, u32[]{:S(2)}) copy-start(f32[4,256,512]{2,1,0:T(8,128)} %param.19) | copy-start | bytes 6291460
  (24 other events, 172.9 us)
Sparse Core Ops, SparseCore 0:
  120.0 30.2 all-reduce.6
  254.1 30.5 all-reduce.8
  388.5 31.2 all-reduce.10
  525.1 35.7 all-reduce.14
  678.0 29.5 all-reduce.12
